TPU v7x, 32 devices: a whole 2x2x4 slice. The times are simulated.
32 devices in a mesh: groups: 2 (over y), strip: 16 (over z, x, core).
Axes of the slice: x: 2, y: 2, z: 4, core: 2. Of those that a mesh axis runs over, the one named last changes fastest.
Arguments:
- bands: bfloat16 [64, 2048], P(('groups', 'strip')), parts along dimension 0, may hold values from -6 to 6
- target: bfloat16 [64, 2048], P('groups', 'strip'), parts along dimension 0, may hold values from -6 to 6
- w_in: bfloat16 [32, 128], replicated, may hold values from -1 to 1
- w_conv: bfloat16 [3, 3, 4, 32, 32], replicated, may hold values from -0.375 to 0.375
- w_track: bfloat16 [3, 3, 128, 128], replicated, may hold values from -0.3125 to 0.3125
- w_out: bfloat16 [128, 32], replicated, may hold values from -0.5 to 0.5
- table: float32 [64, 32], replicated, may hold values from -6 to 6
- dilation: int32 [3], replicated, may hold values from 1 to 8, as said below
- detector: int32 [128], P(('groups', 'strip')), parts along dimension 0, may hold values from 0 to 63
- flags: int32 [128], P(('groups', 'strip')), parts along dimension 0, may hold values 0 or 1
Outputs:
- prediction: bfloat16 [64, 2048], P('groups', 'strip'), parts along dimension 0
- grad_in: float32 [64, 128], P('groups'), parts along dimension 0
- grad_conv: float32 [6, 3, 4, 32, 32], P('groups'), parts along dimension 0
- grad_track: float32 [6, 3, 128, 128], P('groups'), parts along dimension 0
- grad_out: float32 [256, 32], P('groups'), parts along dimension 0
- grad_table: float32 [128, 32], P('groups'), parts along dimension 0
There are 2 independent parts, one for each index of `groups`. A program takes and returns all parts, laid end to end along the dimension named above; an argument that names none is the same for every part. Nothing has to cross between parts.
Inputs may be any that keep to these rules, and one draw needn't show every extreme that they name: `dilation`: each entry is 1 to 8, and one entry equals 8.
All inputs are finite; a program needn't handle non-finite values. No bound on the sum of `flags` on one device may be relied on, other than what follows from the above.
Results may differ from a plain program's by a relative error of at most 0.01.
Values may be sent and summed in bfloat16 or wider, within the bound.
No kernel may reach another device: no remote copies, remote signals or barrier semaphores. Data moves between devices by JAX's collectives and lax.ppermute only.
A program may use at most 64 MiB of HBM per device.

v0:
```python
import math
import jax
import jax.numpy as jnp
from jax import lax
from jax.sharding import PartitionSpec as P


def with_halo(x, sides, width):
    for axis, dim in sides:
        size, length = (lax.axis_size(axis), x.shape[dim])
        up = [(i, (i + 1) % size) for i in range(size - 1)]
        down = [(j, i) for i, j in up]
        last = lax.slice_in_dim(x, length - width, length, axis=dim)
        initial = lax.slice_in_dim(x, 0, width, axis=dim)
        before = lax.ppermute(last, axis, up)
        after = lax.ppermute(initial, axis, down)
        x = jnp.concatenate([before, x, after], axis=dim)
    return x


def silu_slope(preact):
    sigmoid_val = jax.nn.sigmoid(preact)
    return sigmoid_val * (1.0 + preact * (1.0 - sigmoid_val))


def block_diagonal(weight):
    groups = weight.shape[2]
    width = weight.shape[3]
    identity = jnp.eye(groups, dtype=weight.dtype)
    spread = weight[:, :, :, :, None, :] * identity[None, None, :, None, :, None]
    return spread.reshape(3, 3, groups * width, groups * width)


def conv_forward(padded, dense_weight):
    row_count = padded.shape[0] - 2
    col_count = padded.shape[1] - 2
    chan_count = padded.shape[2]
    summed = jnp.zeros((row_count * col_count, dense_weight.shape[3]), jnp.float32)
    for i in range(3):
        for j in range(3):
            window = padded[i : i + row_count, j : j + col_count].reshape(-1, chan_count)
            summed = summed + jnp.dot(
                window, dense_weight[i, j], preferred_element_type=jnp.float32
            )
    return summed.reshape(row_count, col_count, -1)


def conv_transpose(padded_grad, dense_weight):
    row_count = padded_grad.shape[0] - 2
    col_count = padded_grad.shape[1] - 2
    chan_count = padded_grad.shape[2]
    summed = jnp.zeros((row_count * col_count, dense_weight.shape[2]), jnp.float32)
    for i in range(3):
        for j in range(3):
            window = padded_grad[2 - i : 2 - i + row_count, 2 - j : 2 - j + col_count].reshape(
                -1, chan_count
            )
            summed = summed + jnp.dot(
                window, dense_weight[i, j].T, preferred_element_type=jnp.float32
            )
    return summed.reshape(row_count, col_count, -1)


def conv_weight_grad(padded, gradient, groups):
    row_count = gradient.shape[0]
    col_count = gradient.shape[1]
    chan_count = gradient.shape[2]
    width = chan_count // groups
    contract = (((0,), (0,)), ((), ()))
    flat_out = gradient.reshape(-1, chan_count)
    rows_of_taps = []
    for i in range(3):
        taps = []
        for j in range(3):
            window = padded[i : i + row_count, j : j + col_count].reshape(-1, chan_count)
            full = lax.dot_general(window, flat_out, contract, preferred_element_type=jnp.float32)
            taps.append(
                jnp.stack(
                    [
                        full[g * width : (g + 1) * width, g * width : (g + 1) * width]
                        for g in range(groups)
                    ]
                )
            )
        rows_of_taps.append(jnp.stack(taps))
    return jnp.stack(rows_of_taps)


def shifted(source, offset, margin):
    padded = jnp.pad(source, ((margin, margin), (0, 0), (0, 0)))
    return lax.dynamic_slice_in_dim(padded, margin + offset, source.shape[0], 0)


def project_pixels(pixels, w_in):
    flat = jnp.dot(pixels.reshape(-1, pixels.shape[2]), w_in, preferred_element_type=jnp.float32)
    return flat.astype(jnp.bfloat16).reshape(pixels.shape[0], pixels.shape[1], w_in.shape[1])


def column_work(
    features, target_block, w_track, w_out, table, dilation, detector, flags, loss_scale
):
    row_count, col_count, chan_count = features.shape
    band_count = w_out.shape[1]
    layers = w_track.shape[0]
    margin = row_count // 4
    contract = (((0,), (0,)), ((), ()))
    selector = (detector[:, None] == jnp.arange(table.shape[0], dtype=jnp.int32)[None, :]).astype(
        jnp.float32
    )
    flag_values = flags.astype(jnp.float32)
    offsets = flag_values[:, None] * jnp.dot(selector, table, precision=lax.Precision.HIGHEST)
    activations = [features]
    preacts = []
    current = features
    for layer_index in range(layers):
        spacing = dilation[layer_index]
        preact = jnp.zeros((row_count * col_count, chan_count), jnp.float32)
        for tap_index in range(3):
            moved_rows = shifted(current, (tap_index - 1) * spacing, margin)
            preact = preact + jnp.dot(
                moved_rows.reshape(-1, chan_count),
                w_track[layer_index, tap_index],
                preferred_element_type=jnp.float32,
            )
        preact = preact.reshape(row_count, col_count, chan_count)
        current = (current.astype(jnp.float32) + jax.nn.silu(preact)).astype(jnp.bfloat16)
        preacts.append(preact)
        activations.append(current)
    raw_output = (
        jnp.dot(current.reshape(-1, chan_count), w_out, preferred_element_type=jnp.float32).reshape(
            row_count, col_count, band_count
        )
        + offsets[None]
    )
    prediction = raw_output.astype(jnp.bfloat16)
    residue = (
        prediction.astype(jnp.float32)
        - target_block.reshape(row_count, col_count, band_count).astype(jnp.float32)
    ) * loss_scale
    residue_b = residue.astype(jnp.bfloat16)
    grad_out = lax.dot_general(
        current.reshape(-1, chan_count),
        residue_b.reshape(-1, band_count),
        contract,
        preferred_element_type=jnp.float32,
    )
    column_sums = jnp.sum(residue, axis=0) * flag_values[:, None]
    grad_table = jnp.dot(selector.T, column_sums, precision=lax.Precision.HIGHEST)
    backward = jnp.dot(
        residue_b.reshape(-1, band_count), w_out.T, preferred_element_type=jnp.float32
    ).reshape(row_count, col_count, chan_count)
    track_grads = [None] * layers
    for layer_index in reversed(range(layers)):
        spacing = dilation[layer_index]
        gate_grad = (backward * silu_slope(preacts[layer_index])).astype(jnp.bfloat16)
        flat_grad = gate_grad.reshape(-1, chan_count)
        tap_grads = []
        for tap_index in range(3):
            moved_rows = shifted(activations[layer_index], (tap_index - 1) * spacing, margin)
            tap_grads.append(
                lax.dot_general(
                    moved_rows.reshape(-1, chan_count),
                    flat_grad,
                    contract,
                    preferred_element_type=jnp.float32,
                )
            )
            pulled = jnp.dot(
                flat_grad, w_track[layer_index, tap_index].T, preferred_element_type=jnp.float32
            ).reshape(row_count, col_count, chan_count)
            backward = backward + shifted(pulled, (1 - tap_index) * spacing, margin)
        track_grads[layer_index] = jnp.stack(tap_grads)
    return (
        backward.astype(jnp.bfloat16),
        prediction.reshape(row_count, col_count * band_count),
        jnp.stack(track_grads),
        grad_out,
        grad_table,
    )


def body(bands, target, w_in, w_conv, w_track, w_out, table, dilation, detector, flags):
    band_count = w_in.shape[0]
    chan_count = w_in.shape[1]
    groups = w_conv.shape[2]
    device_count = lax.axis_size("strip")
    dense_conv = block_diagonal(w_conv)
    row_count = bands.shape[0]
    col_count = bands.shape[1] // band_count
    pixels = bands.reshape(row_count, col_count, band_count)
    projected = project_pixels(pixels, w_in)
    padded = with_halo(projected, (("strip", 0),), 1)
    padded = jnp.pad(padded, ((0, 0), (1, 1), (0, 0)))
    spatial = conv_forward(padded, dense_conv)
    features = (projected.astype(jnp.float32) + jax.nn.silu(spatial)).astype(jnp.bfloat16)
    feature_cols = lax.all_to_all(features, "strip", split_axis=1, concat_axis=0, tiled=True)
    loss_scale = 1.0 / math.sqrt(feature_cols.shape[0] * feature_cols.shape[1] * device_count)
    feature_grad, prediction, grad_track, grad_out, grad_table = column_work(
        feature_cols, target, w_track, w_out, table, dilation, detector, flags, loss_scale
    )
    local_grad = lax.all_to_all(feature_grad, "strip", split_axis=0, concat_axis=1, tiled=True)
    mixed_grad = (local_grad.astype(jnp.float32) * silu_slope(spatial)).astype(jnp.bfloat16)
    grad_pad = with_halo(mixed_grad, (("strip", 0),), 1)
    grad_pad = jnp.pad(grad_pad, ((0, 0), (1, 1), (0, 0)))
    lifted = (local_grad.astype(jnp.float32) + conv_transpose(grad_pad, dense_conv)).astype(
        jnp.bfloat16
    )
    grad_conv = conv_weight_grad(padded, mixed_grad, groups)
    contract = (((0,), (0,)), ((), ()))
    grad_in = lax.dot_general(
        pixels.reshape(-1, band_count),
        lifted.reshape(-1, chan_count),
        contract,
        preferred_element_type=jnp.float32,
    )
    grad_in, grad_conv, grad_track, grad_out, grad_table = lax.psum(
        (grad_in, grad_conv, grad_track, grad_out, grad_table), "strip"
    )
    return (prediction, grad_in, grad_conv, grad_track, grad_out, grad_table)


def solution(mesh):
    placed = (
        P(("groups", "strip"), None),
        P("groups", "strip"),
        P(),
        P(),
        P(),
        P(),
        P(),
        P(),
        P(("groups", "strip")),
        P(("groups", "strip")),
    )
    return jax.shard_map(
        body,
        mesh=mesh,
        in_specs=placed,
        out_specs=(
            P("groups", "strip"),
            P("groups", None),
            P("groups", None, None, None, None),
            P("groups", None, None, None),
            P("groups", None),
            P("groups", None),
        ),
        check_vma=False,
    )
```

profile of v0, /device:TPU:0, one launch (start us, length us, event | category | flops | bytes accessed | tf_op | source)
XLA Modules:
  0.0 162.6 jit_solution(9685957175195041190)
XLA Ops:
  7.2 0.8 reshape_reshape.4
  8.0 0.8 convolution_convert_fusion
  8.8 1.3 collective-permute-start.1
  10.1 3.0 %collective-permute-start = (bf16[1,64,128]{2,1,0:T(8,128)(2,1)S(1)}, bf16[1,64,128]{2,1,0:T(8,128)(2,1)S(1)}, u32[]{:S(2)}, u32[]{:S(2)}) collective-permute-start(bf16[1,64,128]{2,1,0:T(8,128)(2,1)S(1)} %get-tuple-element.73), channel_id=1, source_target_pairs={{0,1},{1,2},{2,3},{3,4},{4,5},{5,6},{6,7},{7,8},{8,9},{9,10},{10,1... | collective-permute-start | bytes 49160 | tf_op jit(solution)/shard_map/ppermute | solution.py:15
  13.2 0.7 convert_element_type.177
  13.8 1.5 mul.138
  15.3 0.6 mul.139
  16.2 0.2 convolution_multiply_fusion
  17.1 0.1 convolution_add_fusion.21
  17.2 0.1 convolution_add_fusion.20
  17.3 0.1 convolution_add_fusion.19
  17.5 0.1 convolution_add_fusion.18
  17.6 0.1 fusion.5
  17.8 0.6 copy.53
  18.5 8.0 %all-to-all-start = ((bf16[2,64,128]{2,0,1:T(2,128)(2,1)}), bf16[2,64,128]{2,0,1:T(2,128)(2,1)S(1)}, u32[]{:S(2)}, u32[]{:S(2)}) async-start(bf16[2,64,128]{2,0,1:T(2,128)(2,1)} %copy.53), calls=%async_computation | async-start | bytes 65536 | tf_op jit(solution)/shard_map/all_to_all | solution.py:196
  26.4 0.6 fusion.102
  33.9 0.2 convolution_add_fusion.14
  34.1 0.2 add_convert_fusion.3
  34.7 0.2 add_convert_fusion.1
  34.9 0.2 fusion.24
  35.3 0.1 fusion.39
  35.4 0.2 multiply_convert_fusion.3
  35.7 0.1 fusion.34
  35.9 0.2 multiply_convert_fusion.2
  36.2 0.1 fusion.26
  36.4 0.2 convolution_bitcast_fusion.18
  36.6 0.2 convolution_bitcast_fusion.5
  36.8 0.2 convolution_bitcast_fusion.6
  37.0 0.2 convolution_bitcast_fusion.7
  37.2 0.2 convolution_bitcast_fusion.2
  37.3 0.2 convolution_bitcast_fusion.3
  37.5 0.2 convolution_bitcast_fusion.4
  37.7 0.2 convolution_bitcast_fusion.8
  37.9 0.2 convolution_bitcast_fusion.10
  38.1 0.2 fusion.7
  38.3 0.6 copy.73
  38.9 6.0 %all-to-all-start.1 = ((bf16[32,4,128]{2,1,0:T(4,128)(2,1)}), bf16[32,4,128]{2,1,0:T(4,128)(2,1)S(1)}, u32[]{:S(2)}, u32[]{:S(2)}) async-start(bf16[32,4,128]{2,1,0:T(4,128)(2,1)} %copy.73), calls=%async_computation.1 | async-start | bytes 65536 | tf_op jit(solution)/shard_map/all_to_all | solution.py:201
  44.9 0.3 fusion.80
  45.2 0.2 convolution_bitcast_fusion.9
  45.5 0.9 pad_maximum_fusion.1
  46.3 0.7 reshape.252
  47.0 4.5 %all-to-all-done.1 = bf16[32,4,128]{2,1,0:T(4,128)(2,1)S(1)} async-done(((bf16[32,4,128]{2,1,0:T(4,128)(2,1)}), bf16[32,4,128]{2,1,0:T(4,128)(2,1)S(1)}, u32[]{:S(2)}, u32[]{:S(2)}) %all-to-all-start.1) | async-done | bytes 32800 | tf_op jit(solution)/shard_map/all_to_all | solution.py:201
  51.6 0.2 convolution_bitcast_fusion.11
  51.8 0.2 convolution_bitcast_fusion.12
  52.0 0.2 convolution_bitcast_fusion.13
  52.2 0.2 convolution_bitcast_fusion.15
  52.3 0.2 convolution_bitcast_fusion.16
  52.5 0.2 convolution_bitcast_fusion.17
  52.7 1.3 collective-permute-start.3
  54.0 3.0 %collective-permute-start.2 = (bf16[1,64,128]{2,1,0:T(8,128)(2,1)S(1)}, bf16[1,64,128]{2,1,0:T(8,128)(2,1)S(1)}, u32[]{:S(2)}, u32[]{:S(2)}) collective-permute-start(bf16[1,64,128]{2,1,0:T(8,128)(2,1)S(1)} %get-tuple-element.61), channel_id=1, source_target_pairs={{0,1},{1,2},{2,3},{3,4},{4,5},{5,6},{6,7},{7,8},{8,9},{9,10},{10,1... | collective-permute-start | bytes 49160 | tf_op jit(solution)/shard_map/ppermute | solution.py:15
  57.2 0.2 convolution_bitcast_fusion
  57.7 0.2 convolution_bitcast_fusion.14
  58.2 0.2 convolution_bitcast_fusion.1
  58.6 0.9 pad_maximum_fusion
  59.9 0.2 convolution_add_fusion.5
  60.1 0.2 convolution_add_fusion.4
  60.2 0.2 convolution_add_fusion.3
  60.5 0.2 convolution_add_fusion.1
  60.7 0.2 fusion.57
  60.8 0.3 fusion.10
  61.2 59.5 %all-reduce.11 = (f32[32,128]{1,0:T(8,128)}, f32[128,32]{0,1:T(8,128)}, f32[64,32]{0,1:T(8,128)}) all-reduce(f32[32,128]{1,0:T(8,128)S(1)} %fusion.10, f32[128,32]{0,1:T(8,128)S(1)} %convolution_bitcast_fusion.18, f32[64,32]{0,1:T(8,128)S(1)} %fusion.80), channel_id=1, replica_groups=mesh['groups'=2,'strip'=16] {'strip'}, use_global_device_ids=true, to_apply=%region_0.1 | all-reduce | flops 10240 | bytes 81920 | tf_op jit(solution)/shard_map/psum | solution.py:216
  120.7 32.3 %all-reduce.15.cloned.1.call-done = (f32[3,3,4,32,32]{4,3,2,1,0:T(8,128)}, f32[3,3,128,128]{3,2,1,0:T(8,128)}) async-done(((f32[3,3,4,32,32]{4,3,2,1,0:T(8,128)}, f32[3,3,128,128]{3,2,1,0:T(8,128)}), (f32[3,3,4,32,32]{4,3,2,1,0:T(8,128)}, f32[3,3,128,128]{3,2,1,0:T(8,128)})) %all-reduce.15.cloned.1.call-update) | async-done | bytes 737296 | tf_op jit(solution)/shard_map/psum | solution.py:216
  152.9 2.0 %copy.107 = f32[3,3,4,32,32]{4,3,2,1,0:T(8,128)} copy(f32[3,3,4,32,32]{4,3,2,1,0:T(8,128)} %get-tuple-element.100) | data formatting | bytes 294912
  154.9 0.8 copy.108
  (90 shorter events, 4.4 us)
Async XLA Ops:
  7.2 9.0 %copy-start = (f32[64,32]{0,1:T(8,128)S(1)}, f32[64,32]{0,1:T(8,128)}, u32[]{:S(2)}) copy-start(f32[64,32]{0,1:T(8,128)} %param.16) | copy-start | bytes 24580
  8.8 7.6 %collective-permute-start.1 = (bf16[1,64,128]{2,1,0:T(8,128)(2,1)S(1)}, bf16[1,64,128]{2,1,0:T(8,128)(2,1)S(1)}, u32[]{:S(2)}, u32[]{:S(2)}) collective-permute-start(bf16[1,64,128]{2,1,0:T(8,128)(2,1)S(1)} %get-tuple-element.74), channel_id=1, source_target_pairs={{1,0},{2,1},{3,2},{4,3},{5,4},{6,5},{7,6},{8,7},{9,8},{10,9},{11,1... | collective-permute-start | bytes 49160 | tf_op jit(solution)/shard_map/ppermute | solution.py:16
  10.1 6.3 %collective-permute-start = (bf16[1,64,128]{2,1,0:T(8,128)(2,1)S(1)}, bf16[1,64,128]{2,1,0:T(8,128)(2,1)S(1)}, u32[]{:S(2)}, u32[]{:S(2)}) collective-permute-start(bf16[1,64,128]{2,1,0:T(8,128)(2,1)S(1)} %get-tuple-element.73), channel_id=1, source_target_pairs={{0,1},{1,2},{2,3},{3,4},{4,5},{5,6},{6,7},{7,8},{8,9},{9,10},{10,1... | collective-permute-start | bytes 49160 | tf_op jit(solution)/shard_map/ppermute | solution.py:15
  15.3 0.9 copy-start.6
  16.4 10.0 %copy-start.5 = (s32[3]{0:T(128)S(1)}, s32[3]{0:T(128)}, u32[]{:S(2)}) copy-start(s32[3]{0:T(128)} %param.17) | copy-start | bytes 40
  16.5 16.4 %copy-start.3 = (bf16[32,128]{1,0:T(8,128)(2,1)S(1)}, bf16[32,128]{1,0:T(8,128)(2,1)}, u32[]{:S(2)}) copy-start(bf16[32,128]{1,0:T(8,128)(2,1)} %param.11) | copy-start | bytes 24580
  16.8 16.5 %copy-start.1 = (bf16[3,3,128,128]{3,2,1,0:T(8,128)(2,1)S(1)}, bf16[3,3,128,128]{3,2,1,0:T(8,128)(2,1)}, u32[]{:S(2)}) copy-start(bf16[3,3,128,128]{3,2,1,0:T(8,128)(2,1)} %param.14) | copy-start | bytes 884740
  18.5 14.6 %all-to-all-start = ((bf16[2,64,128]{2,0,1:T(2,128)(2,1)}), bf16[2,64,128]{2,0,1:T(2,128)(2,1)S(1)}, u32[]{:S(2)}, u32[]{:S(2)}) async-start(bf16[2,64,128]{2,0,1:T(2,128)(2,1)} %copy.53), calls=%async_computation | async-start | bytes 65536 | tf_op jit(solution)/shard_map/all_to_all | solution.py:196
  33.8 1.1 copy-start.4
  38.9 12.6 %all-to-all-start.1 = ((bf16[32,4,128]{2,1,0:T(4,128)(2,1)}), bf16[32,4,128]{2,1,0:T(4,128)(2,1)S(1)}, u32[]{:S(2)}, u32[]{:S(2)}) async-start(bf16[32,4,128]{2,1,0:T(4,128)(2,1)} %copy.73), calls=%async_computation.1 | async-start | bytes 65536 | tf_op jit(solution)/shard_map/all_to_all | solution.py:201
  44.9 108.0 %all-reduce.15.cloned.1.call-start = ((), (), s32[]{:S(2)}) async-start(), calls=%async_computation.2 | async-start | bytes 2359296 | tf_op jit(solution)/shard_map/psum | solution.py:216
  52.7 6.8 %collective-permute-start.3 = (bf16[1,64,128]{2,1,0:T(8,128)(2,1)S(1)}, bf16[1,64,128]{2,1,0:T(8,128)(2,1)S(1)}, u32[]{:S(2)}, u32[]{:S(2)}) collective-permute-start(bf16[1,64,128]{2,1,0:T(8,128)(2,1)S(1)} %get-tuple-element.62), channel_id=1, source_target_pairs={{1,0},{2,1},{3,2},{4,3},{5,4},{6,5},{7,6},{8,7},{9,8},{10,9},{11,1... | collective-permute-start | bytes 49160 | tf_op jit(solution)/shard_map/ppermute | solution.py:16
  54.0 5.5 %collective-permute-start.2 = (bf16[1,64,128]{2,1,0:T(8,128)(2,1)S(1)}, bf16[1,64,128]{2,1,0:T(8,128)(2,1)S(1)}, u32[]{:S(2)}, u32[]{:S(2)}) collective-permute-start(bf16[1,64,128]{2,1,0:T(8,128)(2,1)S(1)} %get-tuple-element.61), channel_id=1, source_target_pairs={{0,1},{1,2},{2,3},{3,4},{4,5},{5,6},{6,7},{7,8},{8,9},{9,10},{10,1... | collective-permute-start | bytes 49160 | tf_op jit(solution)/shard_map/ppermute | solution.py:15
  152.9 2.0 %copy-start.2 = (f32[3,3,128,128]{3,2,1,0:T(8,128)S(1)}, f32[3,3,128,128]{3,2,1,0:T(8,128)}, u32[]{:S(2)}) copy-start(f32[3,3,128,128]{3,2,1,0:T(8,128)} %get-tuple-element.101) | copy-start | bytes 1769476
Sparse Core Ops, SparseCore 0:
  59.6 93.2 all-reduce.14
where the time goes:
time: 163 us
  blocking collectives  59.5 us (37%)
  waiting for transfers between devices  36.8 us (23%)
  starting transfers between devices  22.6 us (14%)
  between operations  20.5 us (13%)
  matrix products  10.5 us (6%)
  local copies, waits for them, and re-layouts  9.7 us (6%)
  other arithmetic  2.92 us (2%)
    psum x1, blocking collectives, body(): lax.psum((grad_in, grad_conv, grad_track, grad_out, grad_table), 'strip')  59.5 us
    psum x1, waiting for transfers between devices, body(): lax.psum((grad_in, grad_conv, grad_track, grad_out, grad_table), 'strip')  32.3 us
    all_to_all x1, starting transfers between devices, body(): lax.all_to_all(features, 'strip', split_axis=1, concat_axis=0, tiled=True)  7.95 us
    ppermute x2, starting transfers between devices, with_halo(): before = lax.ppermute(last, axis, up)  6.06 us
    all_to_all x1, starting transfers between devices, body(): lax.all_to_all(feature_grad, 'strip', split_axis=0, concat_axis=1, tiled=...  5.97 us
    all_to_all x1, waiting for transfers between devices, body(): lax.all_to_all(feature_grad, 'strip', split_axis=0, concat_axis=1, tiled=...  4.5 us
  transfers between devices with their start and end apart: 7, of which 2 were waited for; matrix products, arithmetic and copies ran while one was open for 6% of the time, Pallas kernels for 0%

commit v1 on v0

--- a/solution.py
+++ b/solution.py
@@ -198,7 +198,12 @@
     feature_grad, prediction, grad_track, grad_out, grad_table = column_work(
         feature_cols, target, w_track, w_out, table, dilation, detector, flags, loss_scale
     )
-    local_grad = lax.all_to_all(feature_grad, "strip", split_axis=0, concat_axis=1, tiled=True)
+    local_grad = jnp.concatenate(
+        lax.all_to_all(
+            jnp.stack(jnp.split(feature_grad, lax.axis_size("strip"), 0), 0), "strip", 0, 0
+        ),
+        axis=1,
+    )
     mixed_grad = (local_grad.astype(jnp.float32) * silu_slope(spatial)).astype(jnp.bfloat16)
     grad_pad = with_halo(mixed_grad, (("strip", 0),), 1)
     grad_pad = jnp.pad(grad_pad, ((0, 0), (1, 1), (0, 0)))

time: 163 us -> 172 us (1.055)
  local copies, waits for them, and re-layouts: 9.7 us -> 18.4 us
    unnamed x16 -> x31, local copies, waits for them, and re-layouts: 2.83 us -> 11.5 us
where the time goes in v1:
time: 172 us; the launch traced here: 171 us
  blocking collectives  59.5 us (35%)
  waiting for transfers between devices  36.8 us (21%)
  starting transfers between devices  22.6 us (13%)
  between operations  20.6 us (12%)
  local copies, waits for them, and re-layouts  18.4 us (11%)
  matrix products  10.5 us (6%)
  other arithmetic  2.9 us (2%)
    psum x1, blocking collectives, body(): lax.psum((grad_in, grad_conv, grad_track, grad_out, grad_table), 'strip')  59.5 us
    psum x1, waiting for transfers between devices, body(): lax.psum((grad_in, grad_conv, grad_track, grad_out, grad_table), 'strip')  32.3 us
    unnamed x31, local copies, waits for them, and re-layouts  11.5 us
    all_to_all x1, starting transfers between devices, body(): lax.all_to_all(features, 'strip', split_axis=1, concat_axis=0, tiled=True)  7.95 us
    ppermute x2, starting transfers between devices, with_halo(): before = lax.ppermute(last, axis, up)  6.06 us
    all_to_all x1, starting transfers between devices, body(): lax.all_to_all(jnp.stack(jnp.split(feature_grad, lax.axis_size('strip'),...  5.97 us
    all_to_all x1, waiting for transfers between devices, body(): lax.all_to_all(jnp.stack(jnp.split(feature_grad, lax.axis_size('strip'),...  4.5 us
  transfers between devices with their start and end apart: 7, of which 2 were waited for; matrix products, arithmetic and copies ran while one was open for 6% of the time, Pallas kernels for 0%

profile of v1, /device:TPU:0, one launch (start us, length us, event | category | flops | bytes accessed | tf_op | source)
XLA Modules:
  0.0 171.3 jit_solution(11528897608488509562)
XLA Ops:
  7.2 0.8 reshape_reshape.4
  8.0 0.8 convolution_convert_fusion
  8.8 1.3 collective-permute-start.1
  10.1 3.0 %collective-permute-start = (bf16[1,64,128]{2,1,0:T(8,128)(2,1)S(1)}, bf16[1,64,128]{2,1,0:T(8,128)(2,1)S(1)}, u32[]{:S(2)}, u32[]{:S(2)}) collective-permute-start(bf16[1,64,128]{2,1,0:T(8,128)(2,1)S(1)} %get-tuple-element.89), channel_id=1, source_target_pairs={{0,1},{1,2},{2,3},{3,4},{4,5},{5,6},{6,7},{7,8},{8,9},{9,10},{10,1... | collective-permute-start | bytes 49160 | tf_op jit(solution)/shard_map/ppermute | solution.py:15
  13.2 0.7 convert_element_type.172
  13.8 1.5 mul.138
  15.3 0.6 mul.139
  16.2 0.2 convolution_multiply_fusion
  17.8 0.6 copy.1152
  18.5 8.0 %all-to-all-start = ((bf16[2,64,128]{2,0,1:T(2,128)(2,1)}), bf16[2,64,128]{2,0,1:T(2,128)(2,1)S(1)}, u32[]{:S(2)}, u32[]{:S(2)}) async-start(bf16[2,64,128]{2,0,1:T(2,128)(2,1)} %copy.1152), calls=%async_computation | async-start | bytes 65536 | tf_op jit(solution)/shard_map/all_to_all | solution.py:196
  26.4 0.6 fusion.102
  34.1 0.2 add_convert_fusion.3
  34.7 0.2 add_convert_fusion.1
  35.4 0.2 multiply_convert_fusion.4
  35.9 0.2 multiply_convert_fusion.3
  36.4 0.2 convolution_bitcast_fusion.18
  36.6 0.2 convolution_bitcast_fusion.5
  36.8 0.2 convolution_bitcast_fusion.6
  37.0 0.2 convolution_bitcast_fusion.7
  37.2 0.2 convolution_bitcast_fusion.2
  37.3 0.2 convolution_bitcast_fusion.3
  37.5 0.2 convolution_bitcast_fusion.4
  37.7 0.2 convolution_bitcast_fusion.8
  37.9 0.2 convolution_bitcast_fusion.10
  38.3 0.6 constant_dynamic-update-slice_fusion.15
  38.9 0.6 constant_dynamic-update-slice_fusion.14
  39.5 0.6 constant_dynamic-update-slice_fusion.13
  40.1 0.6 constant_dynamic-update-slice_fusion.12
  40.6 0.6 constant_dynamic-update-slice_fusion.11
  41.2 0.6 constant_dynamic-update-slice_fusion.10
  41.8 0.6 constant_dynamic-update-slice_fusion.9
  42.4 0.6 constant_dynamic-update-slice_fusion.8
  43.0 0.6 constant_dynamic-update-slice_fusion.7
  43.5 0.6 constant_dynamic-update-slice_fusion.6
  44.1 0.6 constant_dynamic-update-slice_fusion.5
  44.7 0.6 constant_dynamic-update-slice_fusion.4
  45.3 0.6 constant_dynamic-update-slice_fusion.3
  45.9 0.6 constant_dynamic-update-slice_fusion.2
  46.5 0.6 constant_dynamic-update-slice_fusion.1
  47.0 0.6 constant_dynamic-update-slice_fusion
  47.6 6.0 %all-to-all-start.1 = ((bf16[16,2,4,128]{3,2,1,0:T(4,128)(2,1)}), bf16[16,2,4,128]{3,2,1,0:T(4,128)(2,1)S(1)}, u32[]{:S(2)}, u32[]{:S(2)}) async-start(bf16[16,2,4,128]{3,2,1,0:T(4,128)(2,1)} %constant_dynamic-update-slice_fusion), calls=%async_computation.1 | async-start | bytes 65536 | tf_op jit(solution)/shard_map/all_to_all | solution.py:202
  53.6 0.3 fusion.79
  53.9 0.2 convolution_bitcast_fusion.9
  54.2 0.9 pad_maximum_fusion.1
  55.0 0.7 reshape.248
  55.7 4.5 %all-to-all-done.1 = bf16[16,2,4,128]{3,2,1,0:T(4,128)(2,1)S(1)} async-done(((bf16[16,2,4,128]{3,2,1,0:T(4,128)(2,1)}), bf16[16,2,4,128]{3,2,1,0:T(4,128)(2,1)S(1)}, u32[]{:S(2)}, u32[]{:S(2)}) %all-to-all-start.1) | async-done | bytes 32800 | tf_op jit(solution)/shard_map/all_to_all | solution.py:202
  60.3 0.2 convolution_bitcast_fusion.11
  60.5 0.2 convolution_bitcast_fusion.12
  60.7 0.2 convolution_bitcast_fusion.13
  60.9 0.2 convolution_bitcast_fusion.15
  61.1 0.2 convolution_bitcast_fusion.16
  61.3 0.2 convolution_bitcast_fusion.17
  61.5 1.3 collective-permute-start.3
  62.8 3.0 %collective-permute-start.2 = (bf16[1,64,128]{2,1,0:T(8,128)(2,1)S(1)}, bf16[1,64,128]{2,1,0:T(8,128)(2,1)S(1)}, u32[]{:S(2)}, u32[]{:S(2)}) collective-permute-start(bf16[1,64,128]{2,1,0:T(8,128)(2,1)S(1)} %get-tuple-element.61), channel_id=1, source_target_pairs={{0,1},{1,2},{2,3},{3,4},{4,5},{5,6},{6,7},{7,8},{8,9},{9,10},{10,1... | collective-permute-start | bytes 49160 | tf_op jit(solution)/shard_map/ppermute | solution.py:15
  65.9 0.2 convolution_bitcast_fusion
  66.5 0.2 convolution_bitcast_fusion.14
  66.9 0.2 convolution_bitcast_fusion.1
  67.4 0.9 pad_maximum_fusion
  68.9 0.2 convolution_add_fusion.3
  69.6 0.3 fusion.10
  69.9 59.5 %all-reduce.11 = (f32[32,128]{1,0:T(8,128)}, f32[128,32]{0,1:T(8,128)}, f32[64,32]{0,1:T(8,128)}) all-reduce(f32[32,128]{1,0:T(8,128)S(1)} %fusion.10, f32[128,32]{0,1:T(8,128)S(1)} %convolution_bitcast_fusion.18, f32[64,32]{0,1:T(8,128)S(1)} %fusion.79), channel_id=1, replica_groups=mesh['groups'=2,'strip'=16] {'strip'}, use_global_device_ids=true, to_apply=%region_0.1 | all-reduce | flops 10240 | bytes 81920 | tf_op jit(solution)/shard_map/psum | solution.py:221
  129.4 32.3 %all-reduce.15.cloned.1.call-done = (f32[3,3,4,32,32]{4,3,2,1,0:T(8,128)}, f32[3,3,128,128]{3,2,1,0:T(8,128)}) async-done(((f32[3,3,4,32,32]{4,3,2,1,0:T(8,128)}, f32[3,3,128,128]{3,2,1,0:T(8,128)}), (f32[3,3,4,32,32]{4,3,2,1,0:T(8,128)}, f32[3,3,128,128]{3,2,1,0:T(8,128)})) %all-reduce.15.cloned.1.call-update) | async-done | bytes 737296 | tf_op jit(solution)/shard_map/psum | solution.py:221
  161.7 2.0 %copy.1260 = f32[3,3,4,32,32]{4,3,2,1,0:T(8,128)} copy(f32[3,3,4,32,32]{4,3,2,1,0:T(8,128)} %get-tuple-element.116) | data formatting | bytes 294912
  163.6 0.8 copy.1261
  (108 shorter events, 6.7 us)
Async XLA Ops:
  7.2 9.0 %copy-start = (f32[64,32]{0,1:T(8,128)S(1)}, f32[64,32]{0,1:T(8,128)}, u32[]{:S(2)}) copy-start(f32[64,32]{0,1:T(8,128)} %param.16) | copy-start | bytes 24580
  8.8 7.6 %collective-permute-start.1 = (bf16[1,64,128]{2,1,0:T(8,128)(2,1)S(1)}, bf16[1,64,128]{2,1,0:T(8,128)(2,1)S(1)}, u32[]{:S(2)}, u32[]{:S(2)}) collective-permute-start(bf16[1,64,128]{2,1,0:T(8,128)(2,1)S(1)} %get-tuple-element.90), channel_id=1, source_target_pairs={{1,0},{2,1},{3,2},{4,3},{5,4},{6,5},{7,6},{8,7},{9,8},{10,9},{11,1... | collective-permute-start | bytes 49160 | tf_op jit(solution)/shard_map/ppermute | solution.py:16
  10.1 6.3 %collective-permute-start = (bf16[1,64,128]{2,1,0:T(8,128)(2,1)S(1)}, bf16[1,64,128]{2,1,0:T(8,128)(2,1)S(1)}, u32[]{:S(2)}, u32[]{:S(2)}) collective-permute-start(bf16[1,64,128]{2,1,0:T(8,128)(2,1)S(1)} %get-tuple-element.89), channel_id=1, source_target_pairs={{0,1},{1,2},{2,3},{3,4},{4,5},{5,6},{6,7},{7,8},{8,9},{9,10},{10,1... | collective-permute-start | bytes 49160 | tf_op jit(solution)/shard_map/ppermute | solution.py:15
  15.3 0.9 copy-start.6
  16.4 10.0 %copy-start.5 = (s32[3]{0:T(128)S(1)}, s32[3]{0:T(128)}, u32[]{:S(2)}) copy-start(s32[3]{0:T(128)} %param.17) | copy-start | bytes 40
  16.5 16.4 %copy-start.3 = (bf16[32,128]{1,0:T(8,128)(2,1)S(1)}, bf16[32,128]{1,0:T(8,128)(2,1)}, u32[]{:S(2)}) copy-start(bf16[32,128]{1,0:T(8,128)(2,1)} %param.11) | copy-start | bytes 24580
  16.8 16.5 %copy-start.1 = (bf16[3,3,128,128]{3,2,1,0:T(8,128)(2,1)S(1)}, bf16[3,3,128,128]{3,2,1,0:T(8,128)(2,1)}, u32[]{:S(2)}) copy-start(bf16[3,3,128,128]{3,2,1,0:T(8,128)(2,1)} %param.14) | copy-start | bytes 884740
  18.5 14.6 %all-to-all-start = ((bf16[2,64,128]{2,0,1:T(2,128)(2,1)}), bf16[2,64,128]{2,0,1:T(2,128)(2,1)S(1)}, u32[]{:S(2)}, u32[]{:S(2)}) async-start(bf16[2,64,128]{2,0,1:T(2,128)(2,1)} %copy.1152), calls=%async_computation | async-start | bytes 65536 | tf_op jit(solution)/shard_map/all_to_all | solution.py:196
  33.8 1.1 copy-start.4
  47.6 12.6 %all-to-all-start.1 = ((bf16[16,2,4,128]{3,2,1,0:T(4,128)(2,1)}), bf16[16,2,4,128]{3,2,1,0:T(4,128)(2,1)S(1)}, u32[]{:S(2)}, u32[]{:S(2)}) async-start(bf16[16,2,4,128]{3,2,1,0:T(4,128)(2,1)} %constant_dynamic-update-slice_fusion), calls=%async_computation.1 | async-start | bytes 65536 | tf_op jit(solution)/shard_map/all_to_all | solution.py:202
  53.6 108.1 %all-reduce.15.cloned.1.call-start = ((), (), s32[]{:S(2)}) async-start(), calls=%async_computation.2 | async-start | bytes 2359296 | tf_op jit(solution)/shard_map/psum | solution.py:221
  61.5 6.8 %collective-permute-start.3 = (bf16[1,64,128]{2,1,0:T(8,128)(2,1)S(1)}, bf16[1,64,128]{2,1,0:T(8,128)(2,1)S(1)}, u32[]{:S(2)}, u32[]{:S(2)}) collective-permute-start(bf16[1,64,128]{2,1,0:T(8,128)(2,1)S(1)} %get-tuple-element.62), channel_id=1, source_target_pairs={{1,0},{2,1},{3,2},{4,3},{5,4},{6,5},{7,6},{8,7},{9,8},{10,9},{11,1... | collective-permute-start | bytes 49160 | tf_op jit(solution)/shard_map/ppermute | solution.py:16
  62.8 5.5 %collective-permute-start.2 = (bf16[1,64,128]{2,1,0:T(8,128)(2,1)S(1)}, bf16[1,64,128]{2,1,0:T(8,128)(2,1)S(1)}, u32[]{:S(2)}, u32[]{:S(2)}) collective-permute-start(bf16[1,64,128]{2,1,0:T(8,128)(2,1)S(1)} %get-tuple-element.61), channel_id=1, source_target_pairs={{0,1},{1,2},{2,3},{3,4},{4,5},{5,6},{6,7},{7,8},{8,9},{9,10},{10,1... | collective-permute-start | bytes 49160 | tf_op jit(solution)/shard_map/ppermute | solution.py:15
  161.7 2.0 %copy-start.2 = (f32[3,3,128,128]{3,2,1,0:T(8,128)S(1)}, f32[3,3,128,128]{3,2,1,0:T(8,128)}, u32[]{:S(2)}) copy-start(f32[3,3,128,128]{3,2,1,0:T(8,128)} %get-tuple-element.117) | copy-start | bytes 1769476
Sparse Core Ops, SparseCore 0:
  68.4 93.2 all-reduce.14
